TPU v7x, 32 devices: a whole 2x2x4 slice. The times are simulated.
32 devices in a mesh: row: 8 (over y, x, core), col: 4 (over z).
Axes of the slice: x: 2, y: 2, z: 4, core: 2. Of those that a mesh axis runs over, the one named last changes fastest.
Arguments:
- matrix: float32 [9216, 9216], P('row', 'col'), as said below
Outputs:
- factored: float32 [9216, 9216], P('row', 'col')
Inputs may be any that keep to these rules, and one draw needn't show every extreme that they name: `matrix`: Off-diagonal entries are of order one; each diagonal entry lies between 4 * sqrt(256) and 8 * sqrt(256) times that.
All inputs are finite; a program needn't handle non-finite values.
Results may differ from a plain program's by a relative error of at most 0.0001.
Values sent between devices are 32-bit elements; how exact they have to be, the bound alone decides.
No kernel may reach another device: no remote copies, remote signals or barrier semaphores. Data moves between devices by JAX's collectives and lax.ppermute only.
A program may use at most 128 MiB of HBM per device.

v0:
```python
import jax
import jax.numpy as jnp
from jax import lax
from jax.sharding import PartitionSpec as P

B = 256
STEPS = 2


def from_root(array, axis, root):
    mine = lax.axis_index(axis) == root
    return lax.psum(jnp.where(mine, array, jnp.zeros_like(array)), axis)


def mult(left, right):
    return jnp.dot(left, right, precision=lax.Precision.HIGHEST, preferred_element_type=jnp.float32)


def spans(lead, width, extent):
    result = []
    for owner in range(lead // extent, (lead + width - 1) // extent + 1):
        low = max(lead, owner * extent) - owner * extent
        high = min(lead + width, (owner + 1) * extent) - owner * extent
        result.append((owner, low, high))
    return result


def cols_plain(tile, lead, cols):
    pieces = [
        from_root(tile[:, low:high], "col", owner) for owner, low, high in spans(lead, B, cols)
    ]
    return pieces[0]


def rows_joined(stacked, lead, rows):
    pieces = [
        from_root(stacked[low:high], "row", owner) for owner, low, high in spans(lead, B, rows)
    ]
    return jnp.concatenate(pieces, axis=0)


def inverse_of(block, eye):
    inverse = 1.0 / jnp.diagonal(block)
    first = inverse[:, None] * (2.0 * eye - block * inverse[None, :])
    return mult(first, 2.0 * eye - mult(block, first))


def on_device(matrix):
    rows, cols = matrix.shape
    row_ids = lax.axis_index("row") * rows + jnp.arange(rows, dtype=jnp.int32)[:, None]
    col_ids = lax.axis_index("col") * cols + jnp.arange(cols, dtype=jnp.int32)[None, :]
    eye = jnp.eye(B, dtype=jnp.float32)
    tile = matrix
    for step in range(STEPS):
        lead = step * B
        panel = cols_plain(tile, lead, cols)
        joined = rows_joined(jnp.concatenate([tile, panel], axis=1), lead, rows)
        upper = joined[:, :cols]
        lower = mult(panel, inverse_of(joined[:, cols:], eye))
        update = mult(lower, upper)
        picked = jnp.take(lower, jnp.clip(col_ids[0] - lead, 0, B - 1), axis=1)
        below = row_ids >= lead + B
        right = col_ids >= lead + B
        inside = (col_ids >= lead) & (col_ids < lead + B)
        tile = jnp.where(below & right, tile - update, jnp.where(below & inside, picked, tile))
    return tile


def solution(mesh):
    return jax.shard_map(
        on_device,
        mesh=mesh,
        in_specs=(P("row", "col"),),
        out_specs=P("row", "col"),
        check_vma=False,
    )
```

profile of v0, /device:TPU:0, one launch (start us, length us, event | category | flops | bytes accessed | tf_op | source)
XLA Modules:
  0.0 363.7 jit_solution(15044023038616365987)
XLA Ops:
  6.5 0.0 all-reduce.5.cloned.1.call-start
  6.5 2.4 slice_select_fusion.1
  8.9 0.0 all-reduce.5.cloned.1.call-update
  8.9 0.0 all-reduce.7.cloned.1.call-start
  9.0 59.5 %all-reduce.5.cloned.1.call-done = f32[1152,256]{1,0:T(8,128)} async-done(((f32[1152,256]{1,0:T(8,128)}), f32[1152,256]{1,0:T(8,128)}) %all-reduce.5.cloned.1.call-update) | async-done | bytes 1179664 | tf_op jit(solution)/shard_map/psum | solution.py:12
  68.5 3.6 fusion.3
  72.0 0.0 copy-start.1
  72.0 0.0 all-reduce.7.cloned.1.call-update
  72.1 0.0 all-reduce.9.cloned.1.call-start
  72.1 0.6 fusion.37
  72.7 0.6 compare_and_fusion.1
  73.3 0.6 fusion.33
  74.0 62.3 %all-reduce.7.cloned.1.call-done = f32[256,2560]{1,0:T(8,128)} async-done(((f32[256,2560]{1,0:T(8,128)}), f32[256,2560]{1,0:T(8,128)}) %all-reduce.7.cloned.1.call-update) | async-done | bytes 2621456 | tf_op jit(solution)/shard_map/psum | solution.py:12
  136.3 1.0 slice.40
  137.3 2.3 gather_fusion
  139.6 1.5 convolution_subtract_fusion.3
  141.1 1.4 fusion.11
  142.5 0.0 copy-done.1
  142.5 1.1 fusion.51
  143.6 0.4 copy.6
  144.0 8.8 %gather_fusion.2 = f32[2304,1152]{1,0:T(8,128)} fusion(f32[1152,256]{0,1:T(8,128)S(1)} %copy.6, s32[3072]{0:T(1024)S(1)} %pad_clamp_fusion.1), kind=kCustom, calls=%fused_computation.clone | custom fusion | bytes 21242880 | tf_op jit(solution)/shard_map/jit(_take)/gather | solution.py:61
  152.8 0.0 copy-start.3
  152.8 0.0 copy-start.6
  152.8 0.0 copy-start.7
  152.8 0.0 copy-start.9
  152.8 12.7 %copy.7 = f32[2304,1152]{0,1:T(8,128)} copy(f32[2304,1152]{1,0:T(8,128)} %gather_fusion.2) | data formatting | bytes 21233664 | tf_op jit(solution)/shard_map/jit(_take)/gather | solution.py:61
  165.5 0.0 copy-done.3
  165.5 0.0 copy-done.6
  165.5 0.0 copy-done.7
  165.5 0.0 copy-done.9
  165.5 16.1 %fusion.1 = f32[1152,2304]{1,0:T(8,128)S(1)} fusion(f32[1152,2304]{1,0:T(8,128)} %param.3, f32[1152,256]{1,0:T(8,128)S(1)} %fusion.51, f32[2304,1152]{0,1:T(8,128)} %copy.7, pred[2304]{0:T(1024)(128)(4,1)S(1)} %copy-done.3, pred[2304]{0:T(1024)(128)(4,1)S(1)} %copy-done.7, pred[2304]{0:T(1024)(128)(4,1)S(1)} %copy-done.6, pred[1152]{0:T(1024)(128)(4,1)S(1)} %copy-done.9, ...), kind=kOutput, calls=%fused_computation.7 | convolution fusion | flops 8169652224 | bytes 35397504 | tf_op jit(solution)/shard_map/dot_general | solution.py:16
  181.6 0.0 copy-start
  181.6 4.1 %copy-done = f32[1152,2304]{1,0:T(8,128)} copy-done((f32[1152,2304]{1,0:T(8,128)}, f32[1152,2304]{1,0:T(8,128)S(1)}, u32[]{:S(2)}) %copy-start) | copy-done | bytes 10616856
  185.7 1.1 slice_select_fusion
  186.8 0.0 all-reduce.9.cloned.1.call-update
  186.9 0.2 all-reduce.11.cloned.1.call-start
  187.1 55.4 %all-reduce.9.cloned.1.call-done = f32[1152,256]{1,0:T(8,128)} async-done(((f32[1152,256]{1,0:T(8,128)}), f32[1152,256]{1,0:T(8,128)}) %all-reduce.9.cloned.1.call-update) | async-done | bytes 1179664 | tf_op jit(solution)/shard_map/psum | solution.py:12
  242.5 3.6 fusion.2
  246.2 0.0 copy-start.2
  246.2 0.0 all-reduce.11.cloned.1.call-update
  246.2 0.6 fusion.38
  246.8 0.6 fusion.34
  247.4 63.0 %all-reduce.11.cloned.1.call-done = f32[256,2560]{1,0:T(8,128)} async-done(((f32[256,2560]{1,0:T(8,128)}), f32[256,2560]{1,0:T(8,128)}) %all-reduce.11.cloned.1.call-update) | async-done | bytes 2621456 | tf_op jit(solution)/shard_map/psum | solution.py:12
  310.4 1.0 slice.43
  311.4 2.3 gather_fusion.1
  313.7 1.5 convolution_subtract_fusion.2
  315.2 1.4 fusion.8
  316.6 0.0 copy-done.2
  316.6 1.1 fusion.52
  317.7 0.4 copy.8
  318.1 8.9 %gather_fusion.3 = f32[2304,1152]{1,0:T(8,128)} fusion(f32[1152,256]{0,1:T(8,128)S(1)} %copy.8, s32[3072]{0:T(1024)S(1)} %pad_clamp_fusion), kind=kCustom, calls=%fused_computation.1.clone | custom fusion | bytes 21242880 | tf_op jit(solution)/shard_map/jit(_take)/gather | solution.py:61
  327.0 0.0 copy-start.4
  327.0 0.0 copy-start.5
  327.0 0.0 copy-start.8
  327.0 12.7 %copy.9 = f32[2304,1152]{0,1:T(8,128)} copy(f32[2304,1152]{1,0:T(8,128)} %gather_fusion.3) | data formatting | bytes 21233664 | tf_op jit(solution)/shard_map/jit(_take)/gather | solution.py:61
  339.7 0.0 copy-done.4
  339.7 0.0 copy-done.5
  339.7 0.0 copy-done.8
  339.7 17.5 %fusion = f32[1152,2304]{1,0:T(8,128)} fusion(f32[1152,2304]{1,0:T(8,128)} %copy-done, f32[1152,256]{1,0:T(8,128)S(1)} %fusion.52, f32[2304,1152]{0,1:T(8,128)} %copy.9, pred[2304]{0:T(1024)(128)(4,1)S(1)} %compare_and_fusion, pred[2304]{0:T(1024)(128)(4,1)S(1)} %copy-done.5, pred[2304]{0:T(1024)(128)(4,1)S(1)} %copy-done.4, ...), kind=kOutput, calls=%fused_computation.5 | convolution fusion | flops 8169652224 | bytes 35397504 | tf_op jit(solution)/shard_map/dot_general | solution.py:16
  (8 shorter events, 0.1 us)
Async XLA Ops:
  6.5 61.9 %all-reduce.5.cloned.1.call-start = ((), (), s32[]{:S(2)}) async-start(), calls=%async_computation | async-start | bytes 2359296 | tf_op jit(solution)/shard_map/psum | solution.py:12
  8.9 127.4 %all-reduce.7.cloned.1.call-start = ((), (), s32[]{:S(2)}) async-start(), calls=%async_computation.1 | async-start | bytes 5242880 | tf_op jit(solution)/shard_map/psum | solution.py:12
  72.0 70.5 %copy-start.1 = (f32[1152,256]{1,0:T(8,128)S(1)}, f32[1152,256]{1,0:T(8,128)}, u32[]{:S(2)}) copy-start(f32[1152,256]{1,0:T(8,128)} %all-reduce.5.cloned.1.call-done) | copy-start | bytes 3538948
  72.1 170.5 %all-reduce.9.cloned.1.call-start = ((), (), s32[]{:S(2)}) async-start(), calls=%async_computation.2 | async-start | bytes 2359296 | tf_op jit(solution)/shard_map/psum | solution.py:12
  152.8 12.7 %copy-start.3 = (pred[2304]{0:T(1024)(128)(4,1)S(1)}, pred[2304]{0:T(1024)(128)(4,1)}, u32[]{:S(2)}) copy-start(pred[2304]{0:T(1024)(128)(4,1)} %compare_and_fusion.1) | copy-start | bytes 6916
  152.8 12.7 %copy-start.6 = (pred[2304]{0:T(1024)(128)(4,1)S(1)}, pred[2304]{0:T(1024)(128)(4,1)}, u32[]{:S(2)}) copy-start(pred[2304]{0:T(1024)(128)(4,1)} %get-tuple-element.6) | copy-start | bytes 6916
  152.8 12.7 %copy-start.7 = (pred[2304]{0:T(1024)(128)(4,1)S(1)}, pred[2304]{0:T(1024)(128)(4,1)}, u32[]{:S(2)}) copy-start(pred[2304]{0:T(1024)(128)(4,1)} %get-tuple-element.7) | copy-start | bytes 6916
  152.8 12.7 %copy-start.9 = (pred[1152]{0:T(1024)(128)(4,1)S(1)}, pred[1152]{0:T(1024)(128)(4,1)}, u32[]{:S(2)}) copy-start(pred[1152]{0:T(1024)(128)(4,1)} %fusion.37) | copy-start | bytes 3460
  181.6 4.1 %copy-start = (f32[1152,2304]{1,0:T(8,128)}, f32[1152,2304]{1,0:T(8,128)S(1)}, u32[]{:S(2)}) copy-start(f32[1152,2304]{1,0:T(8,128)S(1)} %fusion.1) | copy-start | bytes 31850500
  186.9 123.5 %all-reduce.11.cloned.1.call-start = ((), (), s32[]{:S(2)}) async-start(), calls=%async_computation.3 | async-start | bytes 5242880 | tf_op jit(solution)/shard_map/psum | solution.py:12
  246.2 70.5 %copy-start.2 = (f32[1152,256]{1,0:T(8,128)S(1)}, f32[1152,256]{1,0:T(8,128)}, u32[]{:S(2)}) copy-start(f32[1152,256]{1,0:T(8,128)} %all-reduce.9.cloned.1.call-done) | copy-start | bytes 3538948
  327.0 12.7 %copy-start.4 = (pred[2304]{0:T(1024)(128)(4,1)S(1)}, pred[2304]{0:T(1024)(128)(4,1)}, u32[]{:S(2)}) copy-start(pred[2304]{0:T(1024)(128)(4,1)} %get-tuple-element.8) | copy-start | bytes 6916
  327.0 12.7 %copy-start.5 = (pred[2304]{0:T(1024)(128)(4,1)S(1)}, pred[2304]{0:T(1024)(128)(4,1)}, u32[]{:S(2)}) copy-start(pred[2304]{0:T(1024)(128)(4,1)} %get-tuple-element.9) | copy-start | bytes 6916
  327.0 12.7 %copy-start.8 = (pred[1152]{0:T(1024)(128)(4,1)S(1)}, pred[1152]{0:T(1024)(128)(4,1)}, u32[]{:S(2)}) copy-start(pred[1152]{0:T(1024)(128)(4,1)} %fusion.38) | copy-start | bytes 3460
Sparse Core Ops, SparseCore 0:
  9.7 58.6 all-reduce.4
  72.2 64.0 all-reduce.6
  187.0 55.5 all-reduce.8
  246.3 64.0 all-reduce.10
where the time goes:
time: 365 us; the launch traced here: 364 us
  waiting for transfers between devices  240 us (66%)
  local copies, waits for them, and re-layouts  54.6 us (15%)
  matrix products  41.4 us (11%)
  other arithmetic  13.7 us (4%)
  between operations  13.3 us (4%)
    psum x4, waiting for transfers between devices, from_root(): return lax.psum(jnp.where(mine, array, jnp.zeros_like(array)), axis)  240 us
    gather x4, local copies, waits for them, and re-layouts, on_device(): picked = jnp.take(lower, jnp.clip(col_ids[0] - lead, 0, B - 1), axis=1)  43.1 us
    dot_general x8, matrix products, mult(): jnp.dot(left, right, precision=lax.Precision.HIGHEST, preferred_element_t...  41.4 us
    select_n x4, other arithmetic, from_root(): return lax.psum(jnp.where(mine, array, jnp.zeros_like(array)), axis)  10.7 us
  transfers between devices with their start and end apart: 4, of which 4 were waited for; matrix products, arithmetic and copies ran while one was open for 1% of the time, Pallas kernels for 0%

commit v1 on v0

--- a/solution.py
+++ b/solution.py
@@ -9,7 +9,7 @@
 
 def from_root(array, axis, root):
     mine = lax.axis_index(axis) == root
-    return lax.psum(jnp.where(mine, array, jnp.zeros_like(array)), axis)
+    return jnp.sum(lax.all_gather(jnp.where(mine, array, jnp.zeros_like(array)), axis), axis=0)
 
 
 def mult(left, right):

time: 365 us -> 539 us (1.48)
  waiting for transfers between devices: 240 us -> 393 us
  other arithmetic: 13.7 us -> 34.5 us
    all_gather x0 -> x4, waiting for transfers between devices: none -> 393 us  [from_root(): lax.all_gather(jnp.where(mine, array, jnp.zeros_like(array)), axis)]
    psum x4 -> x0, waiting for transfers between devices: 240 us -> none  [from_root(): return lax.psum(jnp.where(mine, array, jnp.zeros_like(array)), axis)]
    reduce_sum x0 -> x4, other arithmetic: none -> 23 us  [from_root(): jnp.sum(lax.all_gather(jnp.where(mine, array, jnp.zeros_like(array)), axi...]
  transfers between devices with their start and end apart: 4 -> 4, of which waited for: 4 -> 4; matrix products, arithmetic and copies ran while one was open for 1% -> 0% of each run, Pallas kernels for 0% -> 0%
where the time goes in v1:
time: 539 us; the launch traced here: 538 us
  waiting for transfers between devices  393 us (73%)
  local copies, waits for them, and re-layouts  55.5 us (10%)
  matrix products  41.1 us (8%)
  other arithmetic  34.5 us (6%)
  between operations  13.4 us (2%)
    all_gather x4, waiting for transfers between devices, from_root(): lax.all_gather(jnp.where(mine, array, jnp.zeros_like(array)), axis)  393 us
    gather x4, local copies, waits for them, and re-layouts, on_device(): picked = jnp.take(lower, jnp.clip(col_ids[0] - lead, 0, B - 1), axis=1)  43.4 us
    dot_general x8, matrix products, mult(): jnp.dot(left, right, precision=lax.Precision.HIGHEST, preferred_element_t...  41.1 us
    reduce_sum x4, other arithmetic, from_root(): jnp.sum(lax.all_gather(jnp.where(mine, array, jnp.zeros_like(array)), axi...  23 us
    select_n x4, other arithmetic, from_root(): jnp.where(mine, array, jnp.zeros_like(array))  11.4 us
  transfers between devices with their start and end apart: 4, of which 4 were waited for; matrix products, arithmetic and copies ran while one was open for 0% of the time, Pallas kernels for 0%

profile of v1, /device:TPU:0, one launch (start us, length us, event | category | flops | bytes accessed | tf_op | source)
XLA Modules:
  0.0 538.3 jit_solution(17056994639685661695)
XLA Ops:
  6.5 0.0 all-gather.9.cloned.1.call-start
  6.5 2.4 slice_select_fusion.1
  8.9 0.0 all-gather.9.cloned.1.call-update
  8.9 0.0 all-gather.11.cloned.1.call-start
  9.0 92.2 %all-gather.9.cloned.1.call-done = f32[4608,256]{1,0:T(8,128)} async-done(((f32[1152,256]{1,0:T(8,128)}), f32[4608,256]{1,0:T(8,128)}) %all-gather.9.cloned.1.call-update) | async-done | bytes 4718608 | tf_op jit(solution)/shard_map/all_gather | solution.py:12
  101.2 2.8 reduce_sum.36
  104.0 0.0 copy-start.5
  104.0 3.9 fusion.3
  108.0 0.0 copy-done.5
  108.0 0.0 all-gather.11.cloned.1.call-update
  108.0 0.0 all-gather.13.cloned.1.call-start
  108.2 105.9 %all-gather.11.cloned.1.call-done = f32[2048,2560]{1,0:T(8,128)} async-done(((f32[256,2560]{1,0:T(8,128)}), f32[2048,2560]{1,0:T(8,128)}) %all-gather.11.cloned.1.call-update) | async-done | bytes 20971536 | tf_op jit(solution)/shard_map/all_gather | solution.py:12
  214.0 8.7 %reduce_sum.37 = f32[256,2560]{1,0:T(8,128)S(1)} reduce(f32[8,256,2560]{2,1,0:T(8,128)} %bitcast.23, f32[]{:T(128)} %constant.12.clone.1), dimensions={0}, to_apply=%region_1.2 | reduce | flops 4587520 | bytes 23592964 | tf_op jit(solution)/shard_map/reduce_sum | solution.py:12
  222.7 0.0 copy-start.3
  222.7 2.3 gather_fusion
  225.1 0.5 convolution_subtract_fusion.3
  225.6 0.4 fusion.11
  226.0 0.0 copy-done.3
  226.0 3.4 fusion.51
  229.4 1.6 copy.6
  231.0 8.8 %gather_fusion.2 = f32[2304,1152]{1,0:T(8,128)} fusion(f32[1152,256]{0,1:T(8,128)S(1)} %copy.6, s32[3072]{0:T(1024)S(1)} %pad_clamp_fusion.1), kind=kCustom, calls=%fused_computation.clone | custom fusion | bytes 21242880 | tf_op jit(solution)/shard_map/jit(_take)/gather | solution.py:61
  239.8 0.0 copy-start.4
  239.8 12.8 %copy.7 = f32[2304,1152]{0,1:T(8,128)} copy(f32[2304,1152]{1,0:T(8,128)} %gather_fusion.2) | data formatting | bytes 21233664 | tf_op jit(solution)/shard_map/jit(_take)/gather | solution.py:61
  252.6 0.0 copy-done.4
  252.6 15.2 %fusion.1 = f32[1152,2304]{1,0:T(8,128)S(1)} fusion(f32[1152,2304]{1,0:T(8,128)} %param.3, f32[1152,256]{1,0:T(8,128)} %fusion.51, f32[2304,1152]{0,1:T(8,128)} %copy.7, pred[2304]{0:T(1024)(128)(4,1)S(1)} %compare_and_fusion.1, pred[2304]{0:T(1024)(128)(4,1)S(1)} %get-tuple-element.7, pred[2304]{0:T(1024)(128)(4,1)S(1)} %get-tuple-element.6, ...), kind=kOutput, calls=%fused_computation.7 | convolution fusion | flops 8169652224 | bytes 35400704 | tf_op jit(solution)/shard_map/dot_general | solution.py:16
  267.9 0.0 copy-start
  267.9 4.1 copy-done
  272.0 1.1 slice_select_fusion
  273.2 0.0 all-gather.13.cloned.1.call-update
  273.2 0.2 all-gather.15.cloned.1.call-start
  273.4 89.3 %all-gather.13.cloned.1.call-done = f32[4608,256]{1,0:T(8,128)} async-done(((f32[1152,256]{1,0:T(8,128)}), f32[4608,256]{1,0:T(8,128)}) %all-gather.13.cloned.1.call-update) | async-done | bytes 4718608 | tf_op jit(solution)/shard_map/all_gather | solution.py:12
  362.7 2.8 reduce_sum.38
  365.6 0.0 copy-start.6
  365.6 4.0 fusion.2
  369.5 0.0 copy-done.6
  369.5 0.0 all-gather.15.cloned.1.call-update
  369.7 105.9 %all-gather.15.cloned.1.call-done = f32[2048,2560]{1,0:T(8,128)} async-done(((f32[256,2560]{1,0:T(8,128)}), f32[2048,2560]{1,0:T(8,128)}) %all-gather.15.cloned.1.call-update) | async-done | bytes 20971536 | tf_op jit(solution)/shard_map/all_gather | solution.py:12
  475.6 8.7 %reduce_sum.39 = f32[256,2560]{1,0:T(8,128)S(1)} reduce(f32[8,256,2560]{2,1,0:T(8,128)} %bitcast.24, f32[]{:T(128)} %constant.12.clone.1), dimensions={0}, to_apply=%region_3.5 | reduce | flops 4587520 | bytes 23592964 | tf_op jit(solution)/shard_map/reduce_sum | solution.py:12
  484.3 0.0 copy-start.1
  484.3 2.3 gather_fusion.1
  486.7 0.5 convolution_subtract_fusion.2
  487.1 0.4 fusion.8
  487.6 0.0 copy-done.1
  487.6 3.5 fusion.52
  491.0 1.6 copy.8
  492.7 8.9 %gather_fusion.3 = f32[2304,1152]{1,0:T(8,128)} fusion(f32[1152,256]{0,1:T(8,128)S(1)} %copy.8, s32[3072]{0:T(1024)S(1)} %pad_clamp_fusion), kind=kCustom, calls=%fused_computation.1.clone | custom fusion | bytes 21242880 | tf_op jit(solution)/shard_map/jit(_take)/gather | solution.py:61
  501.6 0.0 copy-start.2
  501.6 12.8 %copy.9 = f32[2304,1152]{0,1:T(8,128)} copy(f32[2304,1152]{1,0:T(8,128)} %gather_fusion.3) | data formatting | bytes 21233664 | tf_op jit(solution)/shard_map/jit(_take)/gather | solution.py:61
  514.4 0.0 copy-done.2
  514.4 17.3 %fusion = f32[1152,2304]{1,0:T(8,128)} fusion(f32[1152,2304]{1,0:T(8,128)} %copy-done, f32[1152,256]{1,0:T(8,128)} %fusion.52, f32[2304,1152]{0,1:T(8,128)} %copy.9, pred[2304]{0:T(1024)(128)(4,1)S(1)} %compare_and_fusion, pred[2304]{0:T(1024)(128)(4,1)S(1)} %get-tuple-element.9, pred[2304]{0:T(1024)(128)(4,1)S(1)} %get-tuple-element.8, ...), kind=kOutput, calls=%fused_computation.5 | convolution fusion | flops 8169652224 | bytes 35400704 | tf_op jit(solution)/shard_map/dot_general | solution.py:16
  (15 shorter events, 0.2 us)
Async XLA Ops:
  6.5 94.7 %all-gather.9.cloned.1.call-start = ((), (), s32[]{:S(2)}) async-start(), calls=%async_computation | async-start | bytes 5898240 | tf_op jit(solution)/shard_map/all_gather | solution.py:12
  8.9 205.1 %all-gather.11.cloned.1.call-start = ((), (), s32[]{:S(2)}) async-start(), calls=%async_computation.1 | async-start | bytes 23592960 | tf_op jit(solution)/shard_map/all_gather | solution.py:12
  104.0 3.9 copy-start.5
  108.0 254.7 %all-gather.13.cloned.1.call-start = ((), (), s32[]{:S(2)}) async-start(), calls=%async_computation.2 | async-start | bytes 5898240 | tf_op jit(solution)/shard_map/all_gather | solution.py:12
  222.7 3.3 copy-start.3
  239.8 12.8 %copy-start.4 = (f32[256,2560]{1,0:T(8,128)S(1)}, f32[256,2560]{1,0:T(8,128)}, u32[]{:S(2)}) copy-start(f32[256,2560]{1,0:T(8,128)} %copy-done.3) | copy-start | bytes 7864324
  267.9 4.1 copy-start
  273.2 202.4 %all-gather.15.cloned.1.call-start = ((), (), s32[]{:S(2)}) async-start(), calls=%async_computation.3 | async-start | bytes 23592960 | tf_op jit(solution)/shard_map/all_gather | solution.py:12
  365.6 4.0 copy-start.6
  484.3 3.3 copy-start.1
  501.6 12.8 %copy-start.2 = (f32[256,2560]{1,0:T(8,128)S(1)}, f32[256,2560]{1,0:T(8,128)}, u32[]{:S(2)}) copy-start(f32[256,2560]{1,0:T(8,128)} %copy-done.1) | copy-start | bytes 7864324
Sparse Core Ops, SparseCore 0:
  9.0 92.0 all-gather.8
  108.1 105.8 all-gather.10
  273.3 89.3 all-gather.12
  369.7 105.8 all-gather.14
